TPU v7x, 32 devices: a whole 2x2x4 slice. The times are simulated.
32 devices in a mesh: grp: 2 (over y), ctx: 16 (over z, x, core).
Axes of the slice: x: 2, y: 2, z: 4, core: 2. Of those that a mesh axis runs over, the one named last changes fastest.
Arguments:
- query_rows: bfloat16 [4096, 4096], P(('grp', 'ctx')), parts along dimension 0, may hold values from -6 to 6
- key_rows: bfloat16 [4096, 4096], P(('grp', 'ctx')), parts along dimension 0, may hold values from -6 to 6
- value_rows: bfloat16 [4096, 4096], P(('grp', 'ctx')), parts along dimension 0, may hold values from -6 to 6
- grad_out: bfloat16 [4096, 4096], P(('grp', 'ctx')), parts along dimension 0, may hold values from -6 to 6
- conv_filter: bfloat16 [256, 128], replicated, may hold values from -0.44194174 to 0.44194174
Outputs:
- grad_query: bfloat16 [4096, 4096], P(('grp', 'ctx')), parts along dimension 0
- grad_key: bfloat16 [4096, 4096], P(('grp', 'ctx')), parts along dimension 0
- grad_value: bfloat16 [4096, 4096], P(('grp', 'ctx')), parts along dimension 0
- grad_filter: float32 [512, 128], P(('grp', 'ctx')), parts along dimension 0
There are 2 independent parts, one for each index of `grp`. A program takes and returns all parts, laid end to end along the dimension named above; an argument that names none is the same for every part. Nothing has to cross between parts.
All inputs are finite; a program needn't handle non-finite values.
Results may differ from a plain program's by a relative error of at most 0.005.
Values may be sent and summed in bfloat16 or wider, within the bound.
No kernel may reach another device: no remote copies, remote signals or barrier semaphores. Data moves between devices by JAX's collectives and lax.ppermute only.
A program may use at most 64 MiB of HBM per device.

v0:
```python
import math
import jax
import jax.numpy as jnp
from jax import lax
from jax.sharding import PartitionSpec as P

GSIZE = 16
TAPS = 128


def toeplitz(filter_rows, offsets):
    taps_index = lax.broadcasted_iota(jnp.int32, offsets.shape + (TAPS,), 2)
    selector = (offsets[:, :, None] == taps_index).astype(filter_rows.dtype)
    picked = jnp.einsum("gj,tsj->gts", filter_rows, selector, preferred_element_type=jnp.float32)
    return picked.astype(filter_rows.dtype)


def block_terms(prod_now, prod_before, grad_now, grad_after, filter_rows):
    block_total, block_rows, channels = prod_now.shape
    rim_rows = prod_before.shape[1]
    groups_here = channels // GSIZE
    row_index = lax.broadcasted_iota(jnp.int32, (block_rows, block_rows + rim_rows), 0)
    col_index = lax.broadcasted_iota(jnp.int32, (block_rows, block_rows + rim_rows), 1)
    causal = toeplitz(filter_rows, rim_rows + row_index - col_index)
    future = toeplitz(filter_rows, col_index - row_index)
    extended = jnp.concatenate([prod_before, prod_now], axis=1).reshape(
        block_total, block_rows + rim_rows, groups_here, GSIZE
    )
    grads_ahead = jnp.concatenate([grad_now, grad_after], axis=1).reshape(
        block_total, block_rows + rim_rows, groups_here, GSIZE
    )
    mixed_sum = jnp.einsum("gts,bsgc->btgc", causal, extended, preferred_element_type=jnp.float32)
    back_sum = jnp.einsum("gts,bsgc->btgc", future, grads_ahead, preferred_element_type=jnp.float32)
    grads_here = grad_now.reshape(block_total, block_rows, groups_here, GSIZE)
    pair_sums = jnp.einsum(
        "btgc,bsgc->gts", grads_here, extended, preferred_element_type=jnp.float32
    )
    flattened = pair_sums.reshape(groups_here, block_rows * (block_rows + rim_rows))
    flattened = jnp.pad(flattened, ((0, 0), (0, block_rows)))
    skewed = flattened.reshape(groups_here, block_rows, block_rows + rim_rows + 1)
    picked = skewed[:, :, rim_rows - TAPS + 1 : rim_rows + 1]
    filter_part = jnp.flip(jnp.sum(picked, axis=1), axis=1)
    shape_out = (block_total, block_rows, channels)
    return (mixed_sum.reshape(shape_out), back_sum.reshape(shape_out), filter_part)


def window_terms(prod_now, prod_before, grad_now, grad_after, filter_rows, sub_rows):
    block_total, block_rows, channels = prod_now.shape
    sub_count = block_rows // sub_rows
    prod_full = jnp.concatenate([prod_before, prod_now], axis=1)
    prod_full = prod_full.reshape(block_total, (block_rows + TAPS) // sub_rows, sub_rows, channels)
    grad_full = jnp.concatenate([grad_now, grad_after], axis=1)
    grad_full = grad_full.reshape(block_total, (block_rows + TAPS) // sub_rows, sub_rows, channels)
    before_win = prod_full[:, 0:sub_count]
    after_win = grad_full[:, 1 : 1 + sub_count]
    flat_count = block_total * sub_count
    mixed_sum, back_sum, filter_part = block_terms(
        prod_now,
        before_win.reshape(flat_count, TAPS, channels),
        grad_now,
        after_win.reshape(flat_count, TAPS, channels),
        filter_rows,
    )
    return (mixed_sum, back_sum, filter_part)


def run_blocks(prod_now, prod_before, grad_now, grad_after, filter_rows, sub_rows):
    block_total, block_rows, channels = prod_now.shape
    block_width = min(512, channels)
    block_count = channels // block_width

    def to_blocks(array):
        return jnp.moveaxis(
            array.reshape(array.shape[0], array.shape[1], block_count, block_width), 2, 0
        )

    def from_blocks(array):
        return jnp.moveaxis(array, 0, 2).reshape(block_total, block_rows, channels)

    def one_block(block_items):
        return window_terms(
            block_items[0], block_items[1], block_items[2], block_items[3], block_items[4], sub_rows
        )

    block_items = (
        to_blocks(prod_now),
        to_blocks(prod_before),
        to_blocks(grad_now),
        to_blocks(grad_after),
        filter_rows.reshape(block_count, block_width // GSIZE, TAPS),
    )
    mixed_sum, back_sum, filter_part = lax.map(one_block, block_items)
    return (
        from_blocks(mixed_sum),
        from_blocks(back_sum),
        filter_part.reshape(channels // GSIZE, TAPS),
    )


def shards(query_rows, key_rows, value_rows, grad_out, conv_filter):
    product = (key_rows.astype(jnp.float32) * value_rows.astype(jnp.float32)).astype(jnp.bfloat16)
    gated_grad = (grad_out.astype(jnp.float32) * query_rows.astype(jnp.float32)).astype(
        jnp.bfloat16
    )
    local_rows = product.shape[0]
    moved_prod, moved_grad = (
        lax.all_to_all(product, "ctx", split_axis=1, concat_axis=0, tiled=True),
        lax.all_to_all(gated_grad, "ctx", split_axis=1, concat_axis=0, tiled=True),
    )
    total_rows, channels = moved_prod.shape
    block_total = total_rows // TAPS
    blocks_prod = moved_prod.reshape(block_total, TAPS, channels)
    blocks_grad = moved_grad.reshape(block_total, TAPS, channels)
    zero_block = jnp.zeros((1, TAPS, channels), jnp.bfloat16)
    rows_before = jnp.concatenate([zero_block, blocks_prod[:-1]], axis=0)
    rows_after = jnp.concatenate([blocks_grad[1:], zero_block], axis=0)
    groups_here = channels // GSIZE
    own_filter = lax.dynamic_slice_in_dim(
        conv_filter, lax.axis_index("ctx") * groups_here, groups_here, 0
    )
    mixed_sum, back_sum, filter_part = run_blocks(
        blocks_prod, rows_before, blocks_grad, rows_after, own_filter, TAPS
    )
    mixed_sum = mixed_sum.reshape(total_rows, channels)
    back_sum = back_sum.reshape(total_rows, channels)
    mixed_home, back_home = (
        lax.all_to_all(mixed_sum, "ctx", split_axis=0, concat_axis=1, tiled=True),
        lax.all_to_all(back_sum, "ctx", split_axis=0, concat_axis=1, tiled=True),
    )
    grad_scale = 1.0 / math.sqrt(local_rows * lax.axis_size("ctx") * GSIZE)
    grad_query = (grad_out.astype(jnp.float32) * mixed_home).astype(jnp.bfloat16)
    grad_key = (back_home * value_rows.astype(jnp.float32)).astype(jnp.bfloat16)
    grad_value = (back_home * key_rows.astype(jnp.float32)).astype(jnp.bfloat16)
    return (grad_query, grad_key, grad_value, filter_part * grad_scale)


def solution(mesh):
    return jax.shard_map(
        shards,
        mesh=mesh,
        in_specs=(
            P(("grp", "ctx"), None),
            P(("grp", "ctx"), None),
            P(("grp", "ctx"), None),
            P(("grp", "ctx"), None),
            P(),
        ),
        out_specs=(
            P(("grp", "ctx"), None),
            P(("grp", "ctx"), None),
            P(("grp", "ctx"), None),
            P(("grp", "ctx"), None),
        ),
        check_vma=False,
    )
```

profile of v0, /device:TPU:15, one launch (start us, length us, event | category | flops | bytes accessed | tf_op | source)
XLA Modules:
  0.0 199.6 jit_solution(10627907065178947283)
XLA Ops:
  0.6 0.0 copy-start
  0.6 1.8 fusion.7
  2.5 1.3 copy.47
  3.8 6.5 %all-to-all-start.2 = ((bf16[128,16,256]{0,2,1:T(8,128)(2,1)}), bf16[128,16,256]{0,2,1:T(8,128)(2,1)S(1)}, u32[]{:S(2)}, u32[]{:S(2)}) async-start(bf16[128,16,256]{0,2,1:T(8,128)(2,1)} %bitcast.11), calls=%async_computation.2 | async-start | bytes 2097152 | tf_op jit(solution)/shard_map/all_to_all | solution.py:108
  10.3 0.0 copy-done
  10.3 8.2 %fusion.26 = bf16[16,128,256,1]{2,0,1,3:T(8,128)(2,1)} fusion(s32[128,256]{1,0:T(8,128)S(1)} %iota_subtract_fusion, bf16[256,128]{1,0:T(8,128)(2,1)S(1)} %copy-done, s32[]{:T(128)S(6)} %select_n.3), kind=kOutput, calls=%fused_computation.33 | convolution fusion | flops 138936320 | bytes 1183748 | tf_op jit(solution)/shard_map/while/body/eval_jaxpr/gj,tsj->gts/dot_general | solution.py:14
  18.5 16.7 %all-to-all-done.2 = bf16[128,16,256]{0,2,1:T(8,128)(2,1)S(1)} async-done(((bf16[128,16,256]{0,2,1:T(8,128)(2,1)}), bf16[128,16,256]{0,2,1:T(8,128)(2,1)S(1)}, u32[]{:S(2)}, u32[]{:S(2)}) %all-to-all-start.2) | async-done | bytes 1048608 | tf_op jit(solution)/shard_map/all_to_all | solution.py:108
  35.2 0.1 slice.27
  35.2 0.3 fusion.11
  35.5 2.1 %reshape.111 = bf16[16,2,128,256]{2,1,3,0:T(2,128)(2,1)} reshape(bf16[16,256,256]{1,2,0:T(8,128)(2,1)S(1)} %fusion.11) | data formatting | bytes 4194304 | tf_op jit(solution)/shard_map/while/body/eval_jaxpr/reshape | solution.py:53
  37.6 4.0 %slice.28 = bf16[16,1,128,256]{2,1,3,0:T(2,128)(2,1)S(1)} slice(bf16[16,2,128,256]{2,1,3,0:T(2,128)(2,1)} %reshape.111), slice={[0:16], [1:2], [0:128], [0:256]} | slice | bytes 2097152 | tf_op jit(solution)/shard_map/while/body/eval_jaxpr/slice | solution.py:55
  41.6 0.0 copy-start.4
  41.6 0.2 copy.64
  41.8 1.0 copy-done.4
  42.8 0.7 fusion.20
  43.5 1.6 copy.52
  45.1 4.8 %all-to-all-start.3 = ((f32[16,128,256]{1,2,0:T(8,128)}), f32[16,128,256]{1,2,0:T(8,128)S(1)}, u32[]{:S(2)}, u32[]{:S(2)}) async-start(f32[16,128,256]{1,2,0:T(8,128)} %bitcast.49), calls=%async_computation.3 | async-start | bytes 4194304 | tf_op jit(solution)/shard_map/all_to_all | solution.py:128
  49.9 2.3 %copy.38 = bf16[128,4096]{0,1:T(8,128)(2,1)} copy(bf16[128,4096]{1,0:T(8,128)(2,1)} %param.6) | data formatting | bytes 2097152 | tf_op args[1]
  52.2 2.3 %copy.39 = bf16[128,4096]{0,1:T(8,128)(2,1)} copy(bf16[128,4096]{1,0:T(8,128)(2,1)} %param.7) | data formatting | bytes 2097152 | tf_op args[2]
  54.5 42.9 %all-to-all-done.3 = f32[16,128,256]{1,2,0:T(8,128)S(1)} async-done(((f32[16,128,256]{1,2,0:T(8,128)}), f32[16,128,256]{1,2,0:T(8,128)S(1)}, u32[]{:S(2)}, u32[]{:S(2)}) %all-to-all-start.3) | async-done | bytes 2097184 | tf_op jit(solution)/shard_map/all_to_all | solution.py:128
  97.4 3.6 %fusion.8 = (bf16[128,4096]{0,1:T(8,128)(2,1)}, bf16[128,4096]{0,1:T(8,128)(2,1)}, bf16[128,4096]{0,1:T(8,128)(2,1)}) fusion(bf16[128,4096]{0,1:T(8,128)(2,1)} %copy.38, f32[16,128,256]{1,2,0:T(8,128)S(1)} %all-to-all-done.3, bf16[128,4096]{0,1:T(8,128)(2,1)} %copy.39), kind=kLoop, calls=%fused_computation.17 | loop fusion | flops 4194304 | bytes 7340032 | tf_op jit(solution)/shard_map/convert_element_type | solution.py:133
  100.9 4.8 %all-to-all-start = ((bf16[128,16,256]{0,2,1:T(8,128)(2,1)}), bf16[128,16,256]{0,2,1:T(8,128)(2,1)S(1)}, u32[]{:S(2)}, u32[]{:S(2)}) async-start(bf16[128,16,256]{0,2,1:T(8,128)(2,1)} %bitcast.55), calls=%async_computation | async-start | bytes 2097152 | tf_op jit(solution)/shard_map/all_to_all | solution.py:107
  105.7 0.1 iota_subtract_fusion.1
  105.8 8.2 %fusion.25 = bf16[16,128,256,1]{2,0,1,3:T(8,128)(2,1)} fusion(s32[128,256]{1,0:T(8,128)S(1)} %iota_subtract_fusion.1, bf16[256,128]{1,0:T(8,128)(2,1)S(1)} %copy-done, s32[]{:T(128)S(6)} %select_n.3), kind=kOutput, calls=%fused_computation.32 | convolution fusion | flops 138936320 | bytes 1183748 | tf_op jit(solution)/shard_map/while/body/eval_jaxpr/gj,tsj->gts/dot_general | solution.py:14
  114.0 16.6 %all-to-all-done = bf16[128,16,256]{0,2,1:T(8,128)(2,1)S(1)} async-done(((bf16[128,16,256]{0,2,1:T(8,128)(2,1)}), bf16[128,16,256]{0,2,1:T(8,128)(2,1)S(1)}, u32[]{:S(2)}, u32[]{:S(2)}) %all-to-all-start) | async-done | bytes 1048608 | tf_op jit(solution)/shard_map/all_to_all | solution.py:107
  130.6 0.1 slice.25
  130.7 1.6 fusion.12
  132.2 3.9 %copy.40 = bf16[16,256,256]{2,1,0:T(8,128)(2,1)} copy(bf16[16,256,256]{1,2,0:T(8,128)(2,1)} %fusion.12) | data formatting | bytes 4194304 | tf_op jit(solution)/shard_map/while/body/eval_jaxpr/concatenate | solution.py:50
  136.2 2.3 %slice.26 = bf16[16,1,128,256]{3,2,1,0:T(8,128)(2,1)} slice(bf16[16,2,128,256]{3,2,1,0:T(8,128)(2,1)} %bitcast.52), slice={[0:16], [0:1], [0:128], [0:256]} | slice | bytes 2097152 | tf_op jit(solution)/shard_map/while/body/eval_jaxpr/slice | solution.py:54
  138.5 1.6 copy.41
  140.1 0.0 copy-start.2
  140.1 2.3 %fusion.17 = f32[16,128,16,16]{1,3,0,2:T(8,128)S(1)} fusion(bf16[16,128,256,1]{2,0,1,3:T(8,128)(2,1)} %fusion.25, bf16[16,128,16,16]{1,3,2,0:T(8,128)(2,1)S(1)} %bitcast.46, bf16[16,128,16,16]{1,3,2,0:T(8,128)(2,1)S(1)} %bitcast.53), kind=kOutput, calls=%fused_computation.28 | convolution fusion | flops 272629760 | bytes 5242880 | tf_op jit(solution)/shard_map/while/body/eval_jaxpr/gts,bsgc->btgc/dot_general | solution.py:32
  142.4 0.0 copy-done.2
  142.4 1.6 copy.45
  144.0 4.8 %all-to-all-start.1 = ((f32[16,128,256]{1,2,0:T(8,128)}), f32[16,128,256]{1,2,0:T(8,128)}, u32[]{:S(2)}, u32[]{:S(2)}) async-start(f32[16,128,256]{1,2,0:T(8,128)} %bitcast.48), calls=%async_computation.1 | async-start | bytes 4194304 | tf_op jit(solution)/shard_map/all_to_all | solution.py:127
  148.8 0.0 copy-start.1
  148.8 2.4 %copy.55 = bf16[128,4096]{1,0:T(8,128)(2,1)} copy(bf16[128,4096]{0,1:T(8,128)(2,1)} %get-tuple-element.26) | data formatting | bytes 2097152
  151.2 0.0 copy-done.1
  151.2 1.3 copy.54
  152.5 1.7 fusion.35
  154.2 1.2 copy.65
  155.5 0.1 pad.7
  155.6 3.6 %reshape.113 = f32[16,128,257]{2,1,0:T(8,128)} reshape(f32[16,32896]{1,0:T(8,128)S(1)} %pad.7) | data formatting | bytes 4210688 | tf_op jit(solution)/shard_map/while/body/eval_jaxpr/reshape | solution.py:40
  159.3 1.9 slice_reduce_fusion
  161.2 0.1 rev.5
  161.3 0.6 broadcast_multiply_fusion
  161.9 34.5 %all-to-all-done.1 = f32[16,128,256]{1,2,0:T(8,128)} async-done(((f32[16,128,256]{1,2,0:T(8,128)}), f32[16,128,256]{1,2,0:T(8,128)}, u32[]{:S(2)}, u32[]{:S(2)}) %all-to-all-start.1) | async-done | bytes 2097184 | tf_op jit(solution)/shard_map/all_to_all | solution.py:127
  196.4 0.0 copy-start.3
  196.4 2.0 %copy.46 = f32[128,4096]{1,0:T(8,128)S(1)} copy(f32[128,4096]{0,1:T(8,128)} %bitcast.10) | data formatting | bytes 4194304 | tf_op jit(solution)/shard_map/all_to_all | solution.py:127
  198.4 0.0 copy-done.3
  198.4 1.2 fusion.6
  (2 shorter events, 0.0 us)
Async XLA Ops:
  0.6 9.7 %copy-start = (bf16[256,128]{1,0:T(8,128)(2,1)S(1)}, bf16[256,128]{1,0:T(8,128)(2,1)}, u32[]{:S(2)}) copy-start(bf16[256,128]{1,0:T(8,128)(2,1)} %param.9) | copy-start | bytes 196612
  3.8 31.4 %all-to-all-start.2 = ((bf16[128,16,256]{0,2,1:T(8,128)(2,1)}), bf16[128,16,256]{0,2,1:T(8,128)(2,1)S(1)}, u32[]{:S(2)}, u32[]{:S(2)}) async-start(bf16[128,16,256]{0,2,1:T(8,128)(2,1)} %bitcast.11), calls=%async_computation.2 | async-start | bytes 2097152 | tf_op jit(solution)/shard_map/all_to_all | solution.py:108
  41.6 1.2 copy-start.4
  45.1 52.2 %all-to-all-start.3 = ((f32[16,128,256]{1,2,0:T(8,128)}), f32[16,128,256]{1,2,0:T(8,128)S(1)}, u32[]{:S(2)}, u32[]{:S(2)}) async-start(f32[16,128,256]{1,2,0:T(8,128)} %bitcast.49), calls=%async_computation.3 | async-start | bytes 4194304 | tf_op jit(solution)/shard_map/all_to_all | solution.py:128
  100.9 29.6 %all-to-all-start = ((bf16[128,16,256]{0,2,1:T(8,128)(2,1)}), bf16[128,16,256]{0,2,1:T(8,128)(2,1)S(1)}, u32[]{:S(2)}, u32[]{:S(2)}) async-start(bf16[128,16,256]{0,2,1:T(8,128)(2,1)} %bitcast.55), calls=%async_computation | async-start | bytes 2097152 | tf_op jit(solution)/shard_map/all_to_all | solution.py:107
  140.1 2.3 %copy-start.2 = (bf16[16,1,128,256]{2,3,0,1:T(8,128)(2,1)}, bf16[16,1,128,256]{2,3,0,1:T(8,128)(2,1)S(1)}, u32[]{:S(2)}) copy-start(bf16[16,1,128,256]{2,3,0,1:T(8,128)(2,1)S(1)} %copy.41) | copy-start | bytes 3145732
  144.0 52.4 %all-to-all-start.1 = ((f32[16,128,256]{1,2,0:T(8,128)}), f32[16,128,256]{1,2,0:T(8,128)}, u32[]{:S(2)}, u32[]{:S(2)}) async-start(f32[16,128,256]{1,2,0:T(8,128)} %bitcast.48), calls=%async_computation.1 | async-start | bytes 4194304 | tf_op jit(solution)/shard_map/all_to_all | solution.py:127
  148.8 2.4 %copy-start.1 = (bf16[128,4096]{0,1:T(8,128)(2,1)S(1)}, bf16[128,4096]{0,1:T(8,128)(2,1)}, u32[]{:S(2)}) copy-start(bf16[128,4096]{0,1:T(8,128)(2,1)} %get-tuple-element.36) | copy-start | bytes 3145732
  196.4 2.0 %copy-start.3 = (bf16[128,4096]{1,0:T(8,128)(2,1)S(1)}, bf16[128,4096]{1,0:T(8,128)(2,1)}, u32[]{:S(2)}) copy-start(bf16[128,4096]{1,0:T(8,128)(2,1)} %param.8) | copy-start | bytes 3145732
where the time goes:
time: 200 us
  waiting for transfers between devices  111 us (56%)
  local copies, waits for them, and re-layouts  35 us (18%)
  matrix products  21.1 us (11%)
  starting transfers between devices  21 us (10%)
  other arithmetic  11.1 us (6%)
    all_to_all x1, waiting for transfers between devices, shards(): lax.all_to_all(back_sum, 'ctx', split_axis=0, concat_axis=1, tiled=True)  42.9 us
    all_to_all x1, waiting for transfers between devices, shards(): lax.all_to_all(mixed_sum, 'ctx', split_axis=0, concat_axis=1, tiled=True)  34.5 us
    all_to_all x1, waiting for transfers between devices, shards(): lax.all_to_all(gated_grad, 'ctx', split_axis=1, concat_axis=0, tiled=True)  16.7 us
    all_to_all x1, waiting for transfers between devices, shards(): lax.all_to_all(product, 'ctx', split_axis=1, concat_axis=0, tiled=True)  16.6 us
    dot_general x2, matrix products, toeplitz(): jnp.einsum('gj,tsj->gts', filter_rows, selector, preferred_element_type=j...  16.3 us
    unnamed x16, local copies, waits for them, and re-layouts  10.6 us
    all_to_all x1, starting transfers between devices, shards(): lax.all_to_all(gated_grad, 'ctx', split_axis=1, concat_axis=0, tiled=True)  6.52 us
    all_to_all x1, starting transfers between devices, shards(): lax.all_to_all(back_sum, 'ctx', split_axis=0, concat_axis=1, tiled=True)  4.83 us
  transfers between devices with their start and end apart: 4, of which 4 were waited for; matrix products, arithmetic and copies ran while one was open for 17% of the time, Pallas kernels for 0%

commit v1 on v0

--- a/solution.py
+++ b/solution.py
@@ -124,7 +124,12 @@
     mixed_sum = mixed_sum.reshape(total_rows, channels)
     back_sum = back_sum.reshape(total_rows, channels)
     mixed_home, back_home = (
-        lax.all_to_all(mixed_sum, "ctx", split_axis=0, concat_axis=1, tiled=True),
+        jnp.concatenate(
+            lax.all_to_all(
+                jnp.stack(jnp.split(mixed_sum, lax.axis_size("ctx"), axis=0)), "ctx", 0, 0
+            ),
+            axis=1,
+        ),
         lax.all_to_all(back_sum, "ctx", split_axis=0, concat_axis=1, tiled=True),
     )
     grad_scale = 1.0 / math.sqrt(local_rows * lax.axis_size("ctx") * GSIZE)

time: 200 us -> 210 us (1.050)
  local copies, waits for them, and re-layouts: 35 us -> 44.2 us
    unnamed x16 -> x31, local copies, waits for them, and re-layouts: 10.6 us -> 20.6 us
  transfers between devices with their start and end apart: 4 -> 4, of which waited for: 4 -> 4; matrix products, arithmetic and copies ran while one was open for 17% -> 16% of each run, Pallas kernels for 0% -> 0%
where the time goes in v1:
time: 210 us; the launch traced here: 209 us
  waiting for transfers between devices  111 us (53%)
  local copies, waits for them, and re-layouts  44.2 us (21%)
  matrix products  21.1 us (10%)
  starting transfers between devices  21 us (10%)
  other arithmetic  11.1 us (5%)
    all_to_all x1, waiting for transfers between devices, shards(): lax.all_to_all(back_sum, 'ctx', split_axis=0, concat_axis=1, tiled=True)  42.9 us
    all_to_all x1, waiting for transfers between devices, shards(): lax.all_to_all(jnp.stack(jnp.split(mixed_sum, lax.axis_size('ctx'), axis=...  34.5 us
    unnamed x31, local copies, waits for them, and re-layouts  20.6 us
    all_to_all x1, waiting for transfers between devices, shards(): lax.all_to_all(gated_grad, 'ctx', split_axis=1, concat_axis=0, tiled=True)  16.7 us
    all_to_all x1, waiting for transfers between devices, shards(): lax.all_to_all(product, 'ctx', split_axis=1, concat_axis=0, tiled=True)  16.6 us
    dot_general x2, matrix products, toeplitz(): jnp.einsum('gj,tsj->gts', filter_rows, selector, preferred_element_type=j...  16.3 us
    all_to_all x1, starting transfers between devices, shards(): lax.all_to_all(gated_grad, 'ctx', split_axis=1, concat_axis=0, tiled=True)  6.52 us
    all_to_all x1, starting transfers between devices, shards(): lax.all_to_all(back_sum, 'ctx', split_axis=0, concat_axis=1, tiled=True)  4.83 us
  transfers between devices with their start and end apart: 4, of which 4 were waited for; matrix products, arithmetic and copies ran while one was open for 16% of the time, Pallas kernels for 0%

profile of v1, /device:TPU:15, one launch (start us, length us, event | category | flops | bytes accessed | tf_op | source)
XLA Modules:
  0.0 208.8 jit_solution(13051787608539880969)
XLA Ops:
  0.6 0.0 copy-start
  0.6 1.8 fusion.7
  2.5 1.3 copy.45
  3.8 6.5 %all-to-all-start.2 = ((bf16[128,16,256]{0,2,1:T(8,128)(2,1)}), bf16[128,16,256]{0,2,1:T(8,128)(2,1)S(1)}, u32[]{:S(2)}, u32[]{:S(2)}) async-start(bf16[128,16,256]{0,2,1:T(8,128)(2,1)} %bitcast.26), calls=%async_computation.2 | async-start | bytes 2097152 | tf_op jit(solution)/shard_map/all_to_all | solution.py:108
  10.3 0.0 copy-done
  10.3 8.2 %fusion.26 = bf16[16,128,256,1]{2,0,1,3:T(8,128)(2,1)} fusion(s32[128,256]{1,0:T(8,128)S(1)} %iota_subtract_fusion, bf16[256,128]{1,0:T(8,128)(2,1)S(1)} %copy-done, s32[]{:T(128)S(6)} %select_n.3), kind=kOutput, calls=%fused_computation.33 | convolution fusion | flops 138936320 | bytes 1183748 | tf_op jit(solution)/shard_map/while/body/eval_jaxpr/gj,tsj->gts/dot_general | solution.py:14
  18.5 16.7 %all-to-all-done.2 = bf16[128,16,256]{0,2,1:T(8,128)(2,1)S(1)} async-done(((bf16[128,16,256]{0,2,1:T(8,128)(2,1)}), bf16[128,16,256]{0,2,1:T(8,128)(2,1)S(1)}, u32[]{:S(2)}, u32[]{:S(2)}) %all-to-all-start.2) | async-done | bytes 1048608 | tf_op jit(solution)/shard_map/all_to_all | solution.py:108
  35.2 0.1 slice.43
  35.2 0.3 fusion.11
  35.5 2.1 reshape.147
  37.6 4.0 %slice.44 = bf16[16,1,128,256]{2,1,3,0:T(2,128)(2,1)S(1)} slice(bf16[16,2,128,256]{2,1,3,0:T(2,128)(2,1)} %reshape.147), slice={[0:16], [1:2], [0:128], [0:256]} | slice | bytes 2097152 | tf_op jit(solution)/shard_map/while/body/eval_jaxpr/slice | solution.py:55
  41.6 0.0 copy-start.4
  41.6 0.2 copy.63
  41.8 1.0 copy-done.4
  42.8 0.7 fusion.20
  43.6 1.6 copy.50
  45.1 4.8 %all-to-all-start.3 = ((f32[16,128,256]{1,2,0:T(8,128)}), f32[16,128,256]{1,2,0:T(8,128)S(1)}, u32[]{:S(2)}, u32[]{:S(2)}) async-start(f32[16,128,256]{1,2,0:T(8,128)} %bitcast.63), calls=%async_computation.3 | async-start | bytes 4194304 | tf_op jit(solution)/shard_map/all_to_all | solution.py:133
  50.0 2.3 %copy.37 = bf16[128,4096]{0,1:T(8,128)(2,1)} copy(bf16[128,4096]{1,0:T(8,128)(2,1)} %param.6) | data formatting | bytes 2097152 | tf_op args[1]
  52.2 2.3 %copy.38 = bf16[128,4096]{0,1:T(8,128)(2,1)} copy(bf16[128,4096]{1,0:T(8,128)(2,1)} %param.7) | data formatting | bytes 2097152 | tf_op args[2]
  54.5 42.9 %all-to-all-done.3 = f32[16,128,256]{1,2,0:T(8,128)S(1)} async-done(((f32[16,128,256]{1,2,0:T(8,128)}), f32[16,128,256]{1,2,0:T(8,128)S(1)}, u32[]{:S(2)}, u32[]{:S(2)}) %all-to-all-start.3) | async-done | bytes 2097184 | tf_op jit(solution)/shard_map/all_to_all | solution.py:133
  97.4 3.6 %fusion.8 = (bf16[128,4096]{0,1:T(8,128)(2,1)}, bf16[128,4096]{0,1:T(8,128)(2,1)}, bf16[128,4096]{0,1:T(8,128)(2,1)}) fusion(bf16[128,4096]{0,1:T(8,128)(2,1)} %copy.37, f32[16,128,256]{1,2,0:T(8,128)S(1)} %all-to-all-done.3, bf16[128,4096]{0,1:T(8,128)(2,1)} %copy.38), kind=kLoop, calls=%fused_computation.17 | loop fusion | flops 4194304 | bytes 7340032 | tf_op jit(solution)/shard_map/convert_element_type | solution.py:138
  101.0 4.8 %all-to-all-start = ((bf16[128,16,256]{0,2,1:T(8,128)(2,1)}), bf16[128,16,256]{0,2,1:T(8,128)(2,1)S(1)}, u32[]{:S(2)}, u32[]{:S(2)}) async-start(bf16[128,16,256]{0,2,1:T(8,128)(2,1)} %bitcast.69), calls=%async_computation | async-start | bytes 2097152 | tf_op jit(solution)/shard_map/all_to_all | solution.py:107
  105.7 0.1 iota_subtract_fusion.1
  105.8 8.2 %fusion.25 = bf16[16,128,256,1]{2,0,1,3:T(8,128)(2,1)} fusion(s32[128,256]{1,0:T(8,128)S(1)} %iota_subtract_fusion.1, bf16[256,128]{1,0:T(8,128)(2,1)S(1)} %copy-done, s32[]{:T(128)S(6)} %select_n.3), kind=kOutput, calls=%fused_computation.32 | convolution fusion | flops 138936320 | bytes 1183748 | tf_op jit(solution)/shard_map/while/body/eval_jaxpr/gj,tsj->gts/dot_general | solution.py:14
  114.0 16.6 %all-to-all-done = bf16[128,16,256]{0,2,1:T(8,128)(2,1)S(1)} async-done(((bf16[128,16,256]{0,2,1:T(8,128)(2,1)}), bf16[128,16,256]{0,2,1:T(8,128)(2,1)S(1)}, u32[]{:S(2)}, u32[]{:S(2)}) %all-to-all-start) | async-done | bytes 1048608 | tf_op jit(solution)/shard_map/all_to_all | solution.py:107
  130.6 0.1 slice.41
  130.7 1.6 fusion.12
  132.3 3.9 %copy.39 = bf16[16,256,256]{2,1,0:T(8,128)(2,1)} copy(bf16[16,256,256]{1,2,0:T(8,128)(2,1)} %fusion.12) | data formatting | bytes 4194304 | tf_op jit(solution)/shard_map/while/body/eval_jaxpr/concatenate | solution.py:50
  136.2 2.3 %slice.42 = bf16[16,1,128,256]{3,2,1,0:T(8,128)(2,1)} slice(bf16[16,2,128,256]{3,2,1,0:T(8,128)(2,1)} %bitcast.66), slice={[0:16], [0:1], [0:128], [0:256]} | slice | bytes 2097152 | tf_op jit(solution)/shard_map/while/body/eval_jaxpr/slice | solution.py:54
  138.5 1.6 copy.40
  140.1 0.0 copy-start.2
  140.1 2.3 %fusion.17 = f32[16,128,16,16]{1,3,0,2:T(8,128)S(1)} fusion(bf16[16,128,256,1]{2,0,1,3:T(8,128)(2,1)} %fusion.25, bf16[16,128,16,16]{1,3,2,0:T(8,128)(2,1)S(1)} %bitcast.61, bf16[16,128,16,16]{1,3,2,0:T(8,128)(2,1)S(1)} %bitcast.67), kind=kOutput, calls=%fused_computation.28 | convolution fusion | flops 272629760 | bytes 5242880 | tf_op jit(solution)/shard_map/while/body/eval_jaxpr/gts,bsgc->btgc/dot_general | solution.py:32
  142.4 0.2 fusion.36
  142.7 0.7 constant_dynamic-update-slice_fusion.15
  143.3 0.7 constant_dynamic-update-slice_fusion.14
  144.0 0.7 constant_dynamic-update-slice_fusion.13
  144.6 0.7 constant_dynamic-update-slice_fusion.12
  145.3 0.7 constant_dynamic-update-slice_fusion.11
  146.0 0.7 constant_dynamic-update-slice_fusion.10
  146.7 0.7 constant_dynamic-update-slice_fusion.9
  147.3 0.7 constant_dynamic-update-slice_fusion.8
  148.0 0.7 constant_dynamic-update-slice_fusion.7
  148.6 0.7 constant_dynamic-update-slice_fusion.6
  149.3 0.7 constant_dynamic-update-slice_fusion.5
  150.0 0.7 constant_dynamic-update-slice_fusion.4
  150.6 0.7 constant_dynamic-update-slice_fusion.3
  151.3 0.7 constant_dynamic-update-slice_fusion.2
  152.0 0.7 constant_dynamic-update-slice_fusion.1
  152.6 0.7 constant_dynamic-update-slice_fusion
  153.3 4.8 %all-to-all-start.1 = ((f32[16,128,256]{1,2,0:T(8,128)}), f32[16,128,256]{1,2,0:T(8,128)}, u32[]{:S(2)}, u32[]{:S(2)}) async-start(f32[16,128,256]{1,2,0:T(8,128)} %constant_dynamic-update-slice_fusion), calls=%async_computation.1 | async-start | bytes 4194304 | tf_op jit(solution)/shard_map/all_to_all | solution.py:128
  158.1 2.4 %copy.53 = bf16[128,4096]{1,0:T(8,128)(2,1)} copy(bf16[128,4096]{0,1:T(8,128)(2,1)} %get-tuple-element.26) | data formatting | bytes 2097152
  160.5 0.0 copy-done.1
  160.5 1.3 copy.52
  161.8 1.7 fusion.35
  163.5 1.2 copy.64
  164.8 0.1 pad.7
  164.9 3.6 %reshape.149 = f32[16,128,257]{2,1,0:T(8,128)} reshape(f32[16,32896]{1,0:T(8,128)S(1)} %pad.7) | data formatting | bytes 4210688 | tf_op jit(solution)/shard_map/while/body/eval_jaxpr/reshape | solution.py:40
  168.5 1.9 slice_reduce_fusion
  170.5 0.1 rev.5
  170.6 0.6 broadcast_multiply_fusion
  171.2 34.5 %all-to-all-done.1 = f32[16,128,256]{1,2,0:T(8,128)} async-done(((f32[16,128,256]{1,2,0:T(8,128)}), f32[16,128,256]{1,2,0:T(8,128)}, u32[]{:S(2)}, u32[]{:S(2)}) %all-to-all-start.1) | async-done | bytes 2097184 | tf_op jit(solution)/shard_map/all_to_all | solution.py:128
  205.6 2.0 copy.59
  207.7 0.0 copy-done.3
  207.7 1.2 fusion.6
  (5 shorter events, 0.0 us)
Async XLA Ops:
  0.6 9.7 %copy-start = (bf16[256,128]{1,0:T(8,128)(2,1)S(1)}, bf16[256,128]{1,0:T(8,128)(2,1)}, u32[]{:S(2)}) copy-start(bf16[256,128]{1,0:T(8,128)(2,1)} %param.9) | copy-start | bytes 196612
  3.8 31.4 %all-to-all-start.2 = ((bf16[128,16,256]{0,2,1:T(8,128)(2,1)}), bf16[128,16,256]{0,2,1:T(8,128)(2,1)S(1)}, u32[]{:S(2)}, u32[]{:S(2)}) async-start(bf16[128,16,256]{0,2,1:T(8,128)(2,1)} %bitcast.26), calls=%async_computation.2 | async-start | bytes 2097152 | tf_op jit(solution)/shard_map/all_to_all | solution.py:108
  41.6 1.2 copy-start.4
  45.1 52.2 %all-to-all-start.3 = ((f32[16,128,256]{1,2,0:T(8,128)}), f32[16,128,256]{1,2,0:T(8,128)S(1)}, u32[]{:S(2)}, u32[]{:S(2)}) async-start(f32[16,128,256]{1,2,0:T(8,128)} %bitcast.63), calls=%async_computation.3 | async-start | bytes 4194304 | tf_op jit(solution)/shard_map/all_to_all | solution.py:133
  101.0 29.6 %all-to-all-start = ((bf16[128,16,256]{0,2,1:T(8,128)(2,1)}), bf16[128,16,256]{0,2,1:T(8,128)(2,1)S(1)}, u32[]{:S(2)}, u32[]{:S(2)}) async-start(bf16[128,16,256]{0,2,1:T(8,128)(2,1)} %bitcast.69), calls=%async_computation | async-start | bytes 2097152 | tf_op jit(solution)/shard_map/all_to_all | solution.py:107
  140.1 2.3 %copy-start.2 = (bf16[16,1,128,256]{2,3,0,1:T(8,128)(2,1)}, bf16[16,1,128,256]{2,3,0,1:T(8,128)(2,1)S(1)}, u32[]{:S(2)}) copy-start(bf16[16,1,128,256]{2,3,0,1:T(8,128)(2,1)S(1)} %copy.40) | copy-start | bytes 3145732
  153.3 52.4 %all-to-all-start.1 = ((f32[16,128,256]{1,2,0:T(8,128)}), f32[16,128,256]{1,2,0:T(8,128)}, u32[]{:S(2)}, u32[]{:S(2)}) async-start(f32[16,128,256]{1,2,0:T(8,128)} %constant_dynamic-update-slice_fusion), calls=%async_computation.1 | async-start | bytes 4194304 | tf_op jit(solution)/shard_map/all_to_all | solution.py:128
  158.1 2.4 %copy-start.1 = (bf16[128,4096]{0,1:T(8,128)(2,1)S(1)}, bf16[128,4096]{0,1:T(8,128)(2,1)}, u32[]{:S(2)}) copy-start(bf16[128,4096]{0,1:T(8,128)(2,1)} %get-tuple-element.36) | copy-start | bytes 3145732
  205.6 2.0 copy-start.3
